TPU v7x, 256 devices: a whole 4x4x8 slice. The times are simulated.
256 devices in a mesh: strip: 16 (over z_lo, y, core), tensor: 16 (over x, z_hi).
Axes of the slice: x: 4, y: 4, z: 8 (z_hi: 4, z_lo: 2; z = z_hi * 2 + z_lo), core: 2. Of those that a mesh axis runs over, the one named last changes fastest.
Arguments:
- conv_out: bfloat16 [128, 256, 1536], P('strip', 'tensor'), may hold values from -425 to 425
- out_grad: bfloat16 [128, 256, 1536], P('strip', 'tensor'), may hold values from -6 to 6
- layer_norm_gain: float32 [1536], replicated, may hold values from 0.5 to 2
- layer_norm_bias: float32 [1536], replicated, may hold values from -3 to 3
- w_in: bfloat16 [1536, 6144], P('strip', 'tensor'), may hold values from -0.15625 to 0.15625
- b_in: float32 [6144], P('tensor'), may hold values from -3 to 3
- w_out: bfloat16 [6144, 1536], P('tensor', 'strip'), may hold values from -0.078125 to 0.078125
- layer_scale: float32 [1536], replicated, may hold values from 0.25 to 2
- dw_kernel: float32 [7, 7, 1536], replicated, may hold values from -0.875 to 0.875
Outputs:
- grad_input: bfloat16 [128, 256, 1536], P('strip', 'tensor')
- grad_w_in: float32 [1536, 6144], P('strip', 'tensor')
- grad_w_out: float32 [6144, 1536], P('tensor', 'strip')
All inputs are finite; a program needn't handle non-finite values.
Results may differ from a plain program's by a relative error of at most 0.0063.
Values may be sent and summed in bfloat16 or wider, within the bound.
No kernel may reach another device: no remote copies, remote signals or barrier semaphores. Data moves between devices by JAX's collectives and lax.ppermute only.
A program may use at most 128 MiB of HBM per device.

v0:
```python
import math
import jax
import jax.numpy as jnp
from jax import lax
from jax.sharding import PartitionSpec as P

ln_eps = 1e-06
root_half = 0.7071067811865476
density_norm = 0.3989422804014327


def with_halo(block, sides, width):
    for axis, dim in sides:
        count = lax.axis_size(axis)
        forward = [(i, i + 1) for i in range(count - 1)]
        backward = [(target, source) for source, target in forward]
        low = lax.ppermute(
            lax.slice_in_dim(block, block.shape[dim] - width, None, axis=dim), axis, forward
        )
        high = lax.ppermute(lax.slice_in_dim(block, 0, width, axis=dim), axis, backward)
        block = jnp.concatenate([low, block, high], axis=dim)
    return block


def gelu_value(value):
    return 0.5 * value * (1.0 + lax.erf(value * root_half))


def gelu_slope(value):
    return (
        0.5 * (1.0 + lax.erf(value * root_half))
        + value * jnp.exp(-0.5 * value * value) * density_norm
    )


def apply_layer_norm(flattened_rows):
    centre = jnp.mean(flattened_rows, axis=-1, keepdims=True)
    centred = flattened_rows - centre
    spread = jnp.mean(centred * centred, axis=-1, keepdims=True)
    inverse_deviation = lax.rsqrt(spread + ln_eps)
    return (centred * inverse_deviation, inverse_deviation)


def layer_norm_backward(normed_gradient, centred_input, inverse_deviation, layer_norm_gain):
    gain_scaled = normed_gradient * layer_norm_gain
    first_moment = jnp.mean(gain_scaled, axis=-1, keepdims=True)
    second_moment = jnp.mean(gain_scaled * centred_input, axis=-1, keepdims=True)
    return inverse_deviation * (gain_scaled - first_moment - centred_input * second_moment)


def transpose_conv(padded, dw_kernel, image_height, image_breadth):
    taps = dw_kernel.shape[0]
    total = jnp.zeros((image_height, image_breadth, padded.shape[2]), jnp.float32)
    for row_tap in range(taps):
        for col_tap in range(taps):
            start_row = taps - 1 - row_tap
            start_col = taps - 1 - col_tap
            total = (
                total
                + dw_kernel[row_tap, col_tap]
                * padded[
                    start_row : start_row + image_height, start_col : start_col + image_breadth
                ]
            )
    return total


def body(
    conv_out, out_grad, layer_norm_gain, layer_norm_bias, w_in, b_in, w_out, layer_scale, dw_kernel
):
    tile_rows, tile_cols, channel_count = conv_out.shape
    local_count = tile_rows * tile_cols
    flattened_rows = conv_out.astype(jnp.float32).reshape(local_count, channel_count)
    centred_input, inverse_deviation = apply_layer_norm(flattened_rows)
    normed_output = (centred_input * layer_norm_gain + layer_norm_bias).astype(jnp.bfloat16)
    upstream = out_grad.astype(jnp.float32)
    scaled_grad = (upstream.reshape(local_count, channel_count) * layer_scale).astype(jnp.bfloat16)
    w_in_part, w_out_part = (
        lax.all_gather(w_in, "strip", axis=0, tiled=True),
        lax.all_gather(w_out, "strip", axis=1, tiled=True),
    )
    normed_all, scaled_all = (
        lax.all_gather(normed_output, "tensor", axis=0, tiled=True),
        lax.all_gather(scaled_grad, "tensor", axis=0, tiled=True),
    )
    pre_act = jnp.dot(normed_all, w_in_part, preferred_element_type=jnp.float32) + b_in
    hidden_act = gelu_value(pre_act).astype(jnp.bfloat16)
    back_act = lax.dot_general(
        scaled_all, w_out_part, (((1,), (1,)), ((), ())), preferred_element_type=jnp.float32
    )
    back_pre = (back_act * gelu_slope(pre_act)).astype(jnp.bfloat16)
    grad_in = lax.dot_general(
        normed_all, back_pre, (((0,), (0,)), ((), ())), preferred_element_type=jnp.float32
    )
    grad_out = lax.dot_general(
        hidden_act, scaled_all, (((0,), (0,)), ((), ())), preferred_element_type=jnp.float32
    )
    normed_gradient = lax.psum_scatter(
        lax.dot_general(
            back_pre, w_in_part, (((1,), (1,)), ((), ())), preferred_element_type=jnp.float32
        ).astype(jnp.bfloat16),
        "tensor",
        scatter_dimension=0,
        tiled=True,
    ).astype(jnp.float32)
    summed_in, summed_out = (
        lax.psum_scatter(grad_in, "strip", scatter_dimension=0, tiled=True),
        lax.psum_scatter(grad_out, "strip", scatter_dimension=1, tiled=True),
    )
    total_tokens = local_count * lax.axis_size("strip") * lax.axis_size("tensor")
    factor = 1.0 / math.sqrt(total_tokens)
    convolution_gradient = (
        layer_norm_backward(normed_gradient, centred_input, inverse_deviation, layer_norm_gain)
        .astype(jnp.bfloat16)
        .reshape(tile_rows, tile_cols, channel_count)
    )
    margin = dw_kernel.shape[0] // 2
    padded = with_halo(convolution_gradient, (("strip", 0), ("tensor", 1)), margin)
    grad_input = (
        upstream + transpose_conv(padded.astype(jnp.float32), dw_kernel, tile_rows, tile_cols)
    ).astype(jnp.bfloat16)
    return (grad_input, summed_in * factor, summed_out * factor)


def solution(mesh):
    return jax.shard_map(
        body,
        mesh=mesh,
        in_specs=(
            P("strip", "tensor", None),
            P("strip", "tensor", None),
            P(),
            P(),
            P("strip", "tensor"),
            P("tensor"),
            P("tensor", "strip"),
            P(),
            P(),
        ),
        out_specs=(P("strip", "tensor", None), P("strip", "tensor"), P("tensor", "strip")),
        check_vma=False,
    )
```

profile of v0, /device:TPU:2, one launch (start us, length us, event | category | flops | bytes accessed | tf_op | source)
XLA Modules:
  0.0 560.2 jit_solution(12956353183333648456)
XLA Ops:
  7.2 0.0 all-gather.11.cloned.1.call-start
  7.2 0.7 all-gather.11.cloned.1.call-update
  7.9 0.0 all-gather.9.cloned.1.call-start
  8.0 1.1 convert_reduce_fusion
  9.1 0.1 div.16
  9.2 1.2 multiply_reduce_fusion.1
  10.4 0.1 rsqrt.12
  10.5 2.1 add_convert_fusion
  12.6 0.0 all-gather.9.cloned.1.call-update
  12.6 0.0 all-gather.7.cloned.1.call-start
  12.7 0.7 all-gather.7.cloned.1.call-update
  13.3 0.0 all-gather.5.cloned.1.call-start
  13.4 1.8 fusion.59
  15.2 0.0 all-gather.5.cloned.1.call-update
  15.2 0.0 reduce-scatter.4.cloned.1.call-start
  15.3 32.9 %all-gather.11.cloned.1.call-done = bf16[1536,384]{1,0:T(8,128)(2,1)} async-done(((bf16[96,384]{1,0:T(8,128)(2,1)}), bf16[1536,384]{1,0:T(8,128)(2,1)}) %all-gather.11.cloned.1.call-update) | async-done | bytes 1179664 | tf_op jit(solution)/shard_map/all_gather | solution.py:79
  48.2 100.3 %all-gather.9.cloned.1.call-done = bf16[2048,1536]{1,0:T(8,128)(2,1)} async-done(((bf16[128,1536]{1,0:T(8,128)(2,1)}), bf16[2048,1536]{1,0:T(8,128)(2,1)}) %all-gather.9.cloned.1.call-update) | async-done | bytes 6291472 | tf_op jit(solution)/shard_map/all_gather | solution.py:83
  148.5 8.2 %convolution_add_fusion = f32[2048,384]{1,0:T(8,128)} fusion(bf16[2048,1536]{1,0:T(8,128)(2,1)} %all-gather.9.cloned.1.call-done, bf16[1536,384]{1,0:T(8,128)(2,1)} %all-gather.11.cloned.1.call-done, f32[384]{0:T(512)S(1)} %copy-done.5), kind=kOutput, calls=%fused_computation.10 | convolution fusion | flops 2416705536 | bytes 10618368 | tf_op jit(solution)/shard_map/dot_general | solution.py:86
  156.7 27.4 %all-gather.7.cloned.1.call-done = bf16[384,1536]{0,1:T(8,128)(2,1)} async-done(((bf16[384,96]{0,1:T(8,128)(2,1)}), bf16[384,1536]{0,1:T(8,128)(2,1)}) %all-gather.7.cloned.1.call-update) | async-done | bytes 1179664 | tf_op jit(solution)/shard_map/all_gather | solution.py:80
  184.1 99.5 %all-gather.5.cloned.1.call-done = bf16[2048,1536]{1,0:T(8,128)(2,1)} async-done(((bf16[128,1536]{1,0:T(8,128)(2,1)}), bf16[2048,1536]{1,0:T(8,128)(2,1)}) %all-gather.5.cloned.1.call-update) | async-done | bytes 6291472 | tf_op jit(solution)/shard_map/all_gather | solution.py:84
  283.6 8.3 %fusion.5 = bf16[2048,384]{1,0:T(8,128)(2,1)S(1)} fusion(f32[2048,384]{1,0:T(8,128)} %convolution_add_fusion, bf16[2048,1536]{1,0:T(8,128)(2,1)} %all-gather.5.cloned.1.call-done, bf16[384,1536]{0,1:T(8,128)(2,1)} %all-gather.7.cloned.1.call-done), kind=kOutput, calls=%fused_computation.7 | convolution fusion | flops 2423783424 | bytes 12189696 | tf_op jit(solution)/shard_map/dot_general | solution.py:88
  291.9 1.2 copy-done.6
  293.1 5.4 convolution_convert_fusion
  298.5 0.0 reduce-scatter.4.cloned.1.call-update
  298.6 0.2 reduce-scatter.6.cloned.1.call-start
  298.8 1.2 copy-done.7
  300.0 7.7 %fusion.63 = f32[1536,384]{1,0:T(8,128)} fusion(bf16[2048,1536]{1,0:T(8,128)(2,1)} %all-gather.9.cloned.1.call-done, bf16[2048,384]{1,0:T(8,128)(2,1)S(1)} %copy-done.7), kind=kOutput, calls=%fused_computation.184 | convolution fusion | flops 2415919104 | bytes 10223616 | tf_op jit(solution)/shard_map/dot_general | solution.py:92
  307.6 0.0 reduce-scatter.6.cloned.1.call-update
  307.7 0.0 reduce-scatter.8.cloned.1.call-start
  307.7 9.0 %fusion.6 = f32[384,1536]{0,1:T(8,128)} fusion(bf16[2048,1536]{1,0:T(8,128)(2,1)} %all-gather.5.cloned.1.call-done, f32[2048,384]{1,0:T(8,128)} %convolution_add_fusion), kind=kOutput, calls=%fused_computation.11 | convolution fusion | flops 2419851264 | bytes 11796480 | tf_op jit(solution)/shard_map/dot_general | solution.py:95
  316.7 0.0 reduce-scatter.8.cloned.1.call-update
  316.8 0.8 slice_reduce_fusion.46
  317.6 0.9 slice_reduce_fusion.48
  318.5 0.9 slice_reduce_fusion.47
  319.4 86.1 %reduce-scatter.4.cloned.1.call-done = bf16[128,1536]{1,0:T(8,128)(2,1)} async-done(((bf16[2048,1536]{1,0:T(8,128)(2,1)}), bf16[128,1536]{1,0:T(8,128)(2,1)}) %reduce-scatter.4.cloned.1.call-update) | async-done | bytes 393232 | tf_op jit(solution)/shard_map/reduce_scatter | solution.py:98
  405.5 1.3 fusion.60
  406.8 1.4 multiply_convert_fusion.2
  408.2 1.3 collective-permute-start.1
  409.5 3.0 collective-permute-start
  412.6 61.1 %reduce-scatter.6.cloned.1.call-done = f32[96,384]{1,0:T(8,128)} async-done(((f32[1536,384]{1,0:T(8,128)}), f32[96,384]{1,0:T(8,128)}) %reduce-scatter.6.cloned.1.call-update) | async-done | bytes 147472 | tf_op jit(solution)/shard_map/reduce_scatter | solution.py:107
  473.7 1.6 broadcast_multiply_fusion.1
  475.3 0.1 pad_maximum_fusion.2
  475.4 4.4 collective-permute-start.2
  479.9 4.4 collective-permute-start.3
  484.3 59.4 %reduce-scatter.8.cloned.1.call-done = f32[384,96]{0,1:T(8,128)} async-done(((f32[384,1536]{0,1:T(8,128)}), f32[384,96]{0,1:T(8,128)}) %reduce-scatter.8.cloned.1.call-update) | async-done | bytes 147472 | tf_op jit(solution)/shard_map/reduce_scatter | solution.py:108
  543.6 1.6 broadcast_multiply_fusion
  545.2 0.4 maximum_convert_fusion
  545.6 7.7 %fusion.10 = bf16[8,16,1536]{2,1,0:T(8,128)(2,1)} fusion(f32[14,22,1536]{2,1,0:T(8,128)S(1)} %maximum_convert_fusion, f32[1536]{0:T(1024)} %get-tuple-element.52, f32[1536]{0:T(1024)} %get-tuple-element.53, f32[1536]{0:T(1024)} %get-tuple-element.6, f32[1536]{0:T(1024)} %get-tuple-element.7, f32[1536]{0:T(1024)} %get-tuple-element.8, ...), kind=kLoop, calls=%fused_computation.17 | loop fusion | flops 19660800 | bytes 39622656 | tf_op jit(solution)/shard_map/convert_element_type | solution.py:121
  (22 shorter events, 0.1 us)
Async XLA Ops:
  7.2 141.3 %copy-start.5 = (f32[384]{0:T(512)S(1)}, f32[384]{0:T(512)}, u32[]{:S(2)}) copy-start(f32[384]{0:T(512)} %param.14) | copy-start | bytes 4612
  7.2 41.0 %all-gather.11.cloned.1.call-start = ((), (), s32[]{:S(2)}) async-start(), calls=%async_computation.6 | async-start | bytes 1253376 | tf_op jit(solution)/shard_map/all_gather | solution.py:79
  7.9 140.5 %all-gather.9.cloned.1.call-start = ((), (), s32[]{:S(2)}) async-start(), calls=%async_computation.5 | async-start | bytes 6684672 | tf_op jit(solution)/shard_map/all_gather | solution.py:83
  12.6 171.5 %all-gather.7.cloned.1.call-start = ((), (), s32[]{:S(2)}) async-start(), calls=%async_computation.4 | async-start | bytes 1253376 | tf_op jit(solution)/shard_map/all_gather | solution.py:80
  13.3 270.3 %all-gather.5.cloned.1.call-start = ((), (), s32[]{:S(2)}) async-start(), calls=%async_computation.3 | async-start | bytes 6684672 | tf_op jit(solution)/shard_map/all_gather | solution.py:84
  15.2 390.2 %reduce-scatter.4.cloned.1.call-start = ((), (), s32[]{:S(2)}) async-start(), calls=%async_computation.7 | async-start | bytes 6684672 | tf_op jit(solution)/shard_map/reduce_scatter | solution.py:98
  156.7 136.5 %copy-start.4 = (bf16[1536,384]{1,0:T(8,128)(2,1)S(1)}, bf16[1536,384]{1,0:T(8,128)(2,1)}, u32[]{:S(2)}) copy-start(bf16[1536,384]{1,0:T(8,128)(2,1)} %all-gather.11.cloned.1.call-done) | copy-start | bytes 3538948
  291.9 1.2 copy-start.6
  298.5 1.4 copy-start.7
  298.6 175.1 %reduce-scatter.6.cloned.1.call-start = ((), (), s32[]{:S(2)}) async-start(), calls=%async_computation.8 | async-start | bytes 2506752 | tf_op jit(solution)/shard_map/reduce_scatter | solution.py:107
  307.7 9.1 %copy-start.2 = (f32[7,7,1536]{2,1,0:T(8,128)S(1)}, f32[7,7,1536]{2,1,0:T(8,128)}, u32[]{:S(2)}) copy-start(f32[7,7,1536]{2,1,0:T(8,128)} %param.17) | copy-start | bytes 903172
  307.7 97.8 %copy-start.3 = (f32[1536]{0:T(1024)S(1)}, f32[1536]{0:T(1024)}, u32[]{:S(2)}) copy-start(f32[1536]{0:T(1024)} %param.11) | copy-start | bytes 18436
  307.7 235.9 %reduce-scatter.8.cloned.1.call-start = ((), (), s32[]{:S(2)}) async-start(), calls=%async_computation.9 | async-start | bytes 2506752 | tf_op jit(solution)/shard_map/reduce_scatter | solution.py:108
  316.7 88.7 %copy-start = (bf16[8,16,1536]{2,1,0:T(8,128)(2,1)S(1)}, bf16[8,16,1536]{2,1,0:T(8,128)(2,1)}, u32[]{:S(2)}) copy-start(bf16[8,16,1536]{2,1,0:T(8,128)(2,1)} %param.9) | copy-start | bytes 1179652
  406.8 138.9 %copy-start.1 = (bf16[8,16,1536]{2,1,0:T(8,128)(2,1)S(1)}, bf16[8,16,1536]{2,1,0:T(8,128)(2,1)}, u32[]{:S(2)}) copy-start(bf16[8,16,1536]{2,1,0:T(8,128)(2,1)} %param.10) | copy-start | bytes 1179652
  408.2 67.1 %collective-permute-start.1 = (bf16[3,16,1536]{2,1,0:T(8,128)(2,1)S(1)}, bf16[3,16,1536]{2,1,0:T(8,128)(2,1)S(1)}, u32[]{:S(2)}, u32[]{:S(2)}) collective-permute-start(bf16[3,16,1536]{2,1,0:T(8,128)(2,1)S(1)} %bitcast.29), channel_id=1, source_target_pairs={{16,0},{32,16},{48,32},{64,48},{80,64},{96,80},{112,96},{128,112},... | collective-permute-start | bytes 442376 | tf_op jit(solution)/shard_map/ppermute | solution.py:20
  409.5 65.8 %collective-permute-start = (bf16[3,16,1536]{2,1,0:T(8,128)(2,1)S(1)}, bf16[3,16,1536]{2,1,0:T(8,128)(2,1)S(1)}, u32[]{:S(2)}, u32[]{:S(2)}) collective-permute-start(bf16[3,16,1536]{2,1,0:T(8,128)(2,1)S(1)} %bitcast.28), channel_id=1, source_target_pairs={{0,16},{16,32},{32,48},{48,64},{64,80},{80,96},{96,112},{112,128},... | collective-permute-start | bytes 442376 | tf_op jit(solution)/shard_map/ppermute | solution.py:17
  475.4 69.8 %collective-permute-start.2 = (bf16[14,3,1536]{2,1,0:T(4,128)(2,1)S(1)}, bf16[14,3,1536]{2,1,0:T(4,128)(2,1)S(1)}, u32[]{:S(2)}, u32[]{:S(2)}) collective-permute-start(bf16[14,3,1536]{2,1,0:T(4,128)(2,1)S(1)} %get-tuple-element.54), channel_id=1, source_target_pairs={{0,1},{1,2},{2,3},{3,4},{4,5},{5,6},{6,7},{7,8},{8,9},{9,10},{10,1... | collective-permute-start | bytes 387080 | tf_op jit(solution)/shard_map/ppermute | solution.py:17
  479.9 65.4 %collective-permute-start.3 = (bf16[14,3,1536]{2,1,0:T(4,128)(2,1)S(1)}, bf16[14,3,1536]{2,1,0:T(4,128)(2,1)S(1)}, u32[]{:S(2)}, u32[]{:S(2)}) collective-permute-start(bf16[14,3,1536]{2,1,0:T(4,128)(2,1)S(1)} %get-tuple-element.55), channel_id=1, source_target_pairs={{1,0},{2,1},{3,2},{4,3},{5,4},{6,5},{7,6},{8,7},{9,8},{10,9},{11,1... | collective-permute-start | bytes 387080 | tf_op jit(solution)/shard_map/ppermute | solution.py:20
Sparse Core Ops, SparseCore 0:
  9.9 38.2 all-gather.10
  51.2 97.1 all-gather.8
  150.3 33.7 all-gather.6
  186.4 97.1 all-gather.4
  298.7 106.7 reduce-scatter.3
  407.9 65.7 reduce-scatter.5
  476.2 67.3 reduce-scatter.7
where the time goes:
time: 561 us; the launch traced here: 560 us
  waiting for transfers between devices  468 us (83%)
  matrix products  38.6 us (7%)
  other arithmetic  20.3 us (4%)
  between operations  14.3 us (3%)
  starting transfers between devices  13.6 us (2%)
    all_gather x1, waiting for transfers between devices, body(): lax.all_gather(normed_output, 'tensor', axis=0, tiled=True)  100 us
    all_gather x1, waiting for transfers between devices, body(): lax.all_gather(scaled_grad, 'tensor', axis=0, tiled=True)  99.5 us
    reduce_scatter x1, waiting for transfers between devices, body(): lax.psum_scatter(lax.dot_general(back_pre, w_in_part, (((1,), (1,)), ((),...  86.1 us
    reduce_scatter x1, waiting for transfers between devices, body(): lax.psum_scatter(grad_in, 'strip', scatter_dimension=0, tiled=True)  61.1 us
    reduce_scatter x1, waiting for transfers between devices, body(): lax.psum_scatter(grad_out, 'strip', scatter_dimension=1, tiled=True)  59.4 us
    all_gather x1, waiting for transfers between devices, body(): lax.all_gather(w_in, 'strip', axis=0, tiled=True)  32.9 us
    all_gather x1, waiting for transfers between devices, body(): lax.all_gather(w_out, 'strip', axis=1, tiled=True)  27.4 us
  transfers between devices with their start and end apart: 11, of which 7 were waited for; matrix products, arithmetic and copies ran while one was open for 7% of the time, Pallas kernels for 0%

commit v1 on v0

--- a/solution.py
+++ b/solution.py
@@ -81,7 +81,15 @@
     )
     normed_all, scaled_all = (
         lax.all_gather(normed_output, "tensor", axis=0, tiled=True),
-        lax.all_gather(scaled_grad, "tensor", axis=0, tiled=True),
+        jnp.concatenate(
+            lax.all_to_all(
+                jnp.stack(lax.axis_size("tensor") * [scaled_grad]),
+                axis_name="tensor",
+                split_axis=0,
+                concat_axis=0,
+            ),
+            axis=0,
+        ),
     )
     pre_act = jnp.dot(normed_all, w_in_part, preferred_element_type=jnp.float32) + b_in
     hidden_act = gelu_value(pre_act).astype(jnp.bfloat16)

time: 561 us -> 566 us (level)
  starting transfers between devices: 13.6 us -> 23.5 us
    all_gather x1 -> x0, waiting for transfers between devices: 99.5 us -> none  [body(): lax.all_gather(scaled_grad, 'tensor', axis=0, tiled=True)]
    all_gather x1, waiting for transfers between devices: 100 us -> 168 us  [body(): lax.all_gather(normed_output, 'tensor', axis=0, tiled=True)]
    all_gather x1, waiting for transfers between devices: 32.9 us -> 54.9 us  [body(): lax.all_gather(w_in, 'strip', axis=0, tiled=True)]
    all_to_all x0 -> x1, starting transfers between devices: none -> 11.6 us  [body(): lax.all_to_all(jnp.stack(lax.axis_size('tensor') * [scaled_grad]), axis_n...]
  transfers between devices with their start and end apart: 11 -> 11, of which waited for: 7 -> 6; matrix products, arithmetic and copies ran while one was open for 7% -> 7% of each run, Pallas kernels for 0% -> 0%
where the time goes in v1:
time: 566 us
  waiting for transfers between devices  464 us (82%)
  matrix products  38.4 us (7%)
  starting transfers between devices  23.5 us (4%)
  other arithmetic  19.6 us (3%)
  between operations  14.3 us (3%)
  local copies, waits for them, and re-layouts  6.08 us (1%)
    all_gather x1, waiting for transfers between devices, body(): lax.all_gather(normed_output, 'tensor', axis=0, tiled=True)  168 us
    reduce_scatter x1, waiting for transfers between devices, body(): lax.psum_scatter(lax.dot_general(back_pre, w_in_part, (((1,), (1,)), ((),...  89.5 us
    reduce_scatter x1, waiting for transfers between devices, body(): lax.psum_scatter(grad_in, 'strip', scatter_dimension=0, tiled=True)  63.1 us
    reduce_scatter x1, waiting for transfers between devices, body(): lax.psum_scatter(grad_out, 'strip', scatter_dimension=1, tiled=True)  59.4 us
    all_gather x1, waiting for transfers between devices, body(): lax.all_gather(w_in, 'strip', axis=0, tiled=True)  54.9 us
    all_gather x1, waiting for transfers between devices, body(): lax.all_gather(w_out, 'strip', axis=1, tiled=True)  27.4 us
    all_to_all x1, starting transfers between devices, body(): lax.all_to_all(jnp.stack(lax.axis_size('tensor') * [scaled_grad]), axis_n...  11.6 us
  transfers between devices with their start and end apart: 11, of which 6 were waited for; matrix products, arithmetic and copies ran while one was open for 7% of the time, Pallas kernels for 0%

profile of v1, /device:TPU:2, one launch (start us, length us, event | category | flops | bytes accessed | tf_op | source)
XLA Modules:
  0.0 565.8 jit_solution(8753625035293483209)
XLA Ops:
  7.2 0.0 all-gather.8.cloned.1.call-start
  7.2 0.7 all-gather.8.cloned.1.call-update
  7.9 0.0 all-gather.6.cloned.1.call-start
  7.9 1.1 convert_reduce_fusion
  9.1 0.1 div.16
  9.2 1.2 multiply_reduce_fusion.1
  10.4 0.1 rsqrt.12
  10.5 2.1 add_convert_fusion
  12.6 0.0 all-gather.6.cloned.1.call-update
  12.6 1.1 fusion.59
  13.7 3.3 stack.2
  17.0 11.6 %all-to-all-start = ((bf16[16,128,1536]{2,1,0:T(8,128)(2,1)}), bf16[16,128,1536]{2,1,0:T(8,128)(2,1)}, u32[]{:S(2)}, u32[]{:S(2)}) async-start(bf16[16,128,1536]{2,1,0:T(8,128)(2,1)} %stack.2), calls=%async_computation | async-start | bytes 12582912 | tf_op jit(solution)/shard_map/all_to_all | solution.py:85
  28.6 0.0 all-gather.4.cloned.1.call-start
  28.6 0.7 all-gather.4.cloned.1.call-update
  29.3 0.0 reduce-scatter.4.cloned.1.call-start
  29.3 54.9 %all-gather.8.cloned.1.call-done = bf16[1536,384]{1,0:T(8,128)(2,1)} async-done(((bf16[96,384]{1,0:T(8,128)(2,1)}), bf16[1536,384]{1,0:T(8,128)(2,1)}) %all-gather.8.cloned.1.call-update) | async-done | bytes 1179664 | tf_op jit(solution)/shard_map/all_gather | solution.py:79
  84.2 168.2 %all-gather.6.cloned.1.call-done = bf16[2048,1536]{1,0:T(8,128)(2,1)} async-done(((bf16[128,1536]{1,0:T(8,128)(2,1)}), bf16[2048,1536]{1,0:T(8,128)(2,1)}) %all-gather.6.cloned.1.call-update) | async-done | bytes 6291472 | tf_op jit(solution)/shard_map/all_gather | solution.py:83
  252.5 8.2 %convolution_add_fusion = f32[2048,384]{1,0:T(8,128)} fusion(bf16[2048,1536]{1,0:T(8,128)(2,1)} %all-gather.6.cloned.1.call-done, bf16[1536,384]{1,0:T(8,128)(2,1)} %all-gather.8.cloned.1.call-done, f32[384]{0:T(512)S(1)} %copy-done.5), kind=kOutput, calls=%fused_computation.10 | convolution fusion | flops 2416705536 | bytes 10618368 | tf_op jit(solution)/shard_map/dot_general | solution.py:94
  260.7 27.4 %all-gather.4.cloned.1.call-done = bf16[384,1536]{0,1:T(8,128)(2,1)} async-done(((bf16[384,96]{0,1:T(8,128)(2,1)}), bf16[384,1536]{0,1:T(8,128)(2,1)}) %all-gather.4.cloned.1.call-update) | async-done | bytes 1179664 | tf_op jit(solution)/shard_map/all_gather | solution.py:80
  288.1 8.4 %fusion.5 = bf16[2048,384]{1,0:T(8,128)(2,1)S(1)} fusion(f32[2048,384]{1,0:T(8,128)} %convolution_add_fusion, bf16[2048,1536]{1,0:T(8,128)(2,1)} %bitcast.1, bf16[384,1536]{0,1:T(8,128)(2,1)} %all-gather.4.cloned.1.call-done), kind=kOutput, calls=%fused_computation.7 | convolution fusion | flops 2423783424 | bytes 12189696 | tf_op jit(solution)/shard_map/dot_general | solution.py:96
  296.5 5.4 convolution_convert_fusion
  301.9 0.0 reduce-scatter.4.cloned.1.call-update
  301.9 0.2 reduce-scatter.6.cloned.1.call-start
  302.1 7.7 %fusion.63 = f32[1536,384]{1,0:T(8,128)} fusion(bf16[2048,1536]{1,0:T(8,128)(2,1)} %all-gather.6.cloned.1.call-done, bf16[2048,384]{1,0:T(8,128)(2,1)S(1)} %fusion.5), kind=kOutput, calls=%fused_computation.184 | convolution fusion | flops 2415919104 | bytes 10223616 | tf_op jit(solution)/shard_map/dot_general | solution.py:100
  309.8 0.0 reduce-scatter.6.cloned.1.call-update
  309.9 0.0 copy-start.2
  309.9 0.0 copy-start.3
  309.9 0.0 reduce-scatter.8.cloned.1.call-start
  309.9 8.7 %fusion.6 = f32[384,1536]{0,1:T(8,128)} fusion(bf16[2048,1536]{1,0:T(8,128)(2,1)} %bitcast.1, f32[2048,384]{1,0:T(8,128)} %convolution_add_fusion), kind=kOutput, calls=%fused_computation.11 | convolution fusion | flops 2419851264 | bytes 11796480 | tf_op jit(solution)/shard_map/dot_general | solution.py:103
  318.6 0.0 reduce-scatter.8.cloned.1.call-update
  318.7 0.8 slice_reduce_fusion.46
  319.5 0.9 slice_reduce_fusion.48
  320.4 0.9 slice_reduce_fusion.47
  321.3 89.5 %reduce-scatter.4.cloned.1.call-done = bf16[128,1536]{1,0:T(8,128)(2,1)} async-done(((bf16[2048,1536]{1,0:T(8,128)(2,1)}), bf16[128,1536]{1,0:T(8,128)(2,1)}) %reduce-scatter.4.cloned.1.call-update) | async-done | bytes 393232 | tf_op jit(solution)/shard_map/reduce_scatter | solution.py:106
  410.8 1.3 fusion.60
  412.1 0.0 copy-start.1
  412.1 1.4 multiply_convert_fusion.2
  413.5 1.3 collective-permute-start
  414.8 1.3 collective-permute-start.1
  416.1 63.1 %reduce-scatter.6.cloned.1.call-done = f32[96,384]{1,0:T(8,128)} async-done(((f32[1536,384]{1,0:T(8,128)}), f32[96,384]{1,0:T(8,128)}) %reduce-scatter.6.cloned.1.call-update) | async-done | bytes 147472 | tf_op jit(solution)/shard_map/reduce_scatter | solution.py:115
  479.2 1.6 broadcast_multiply_fusion.1
  480.8 0.1 pad_maximum_fusion.2
  480.9 4.6 collective-permute-start.2
  485.6 4.2 collective-permute-start.3
  489.8 59.4 %reduce-scatter.8.cloned.1.call-done = f32[384,96]{0,1:T(8,128)} async-done(((f32[384,1536]{0,1:T(8,128)}), f32[384,96]{0,1:T(8,128)}) %reduce-scatter.8.cloned.1.call-update) | async-done | bytes 147472 | tf_op jit(solution)/shard_map/reduce_scatter | solution.py:116
  549.3 1.6 broadcast_multiply_fusion
  550.8 0.4 maximum_convert_fusion
  551.2 7.7 %fusion.10 = bf16[8,16,1536]{2,1,0:T(8,128)(2,1)} fusion(f32[14,22,1536]{2,1,0:T(8,128)S(1)} %maximum_convert_fusion, f32[1536]{0:T(1024)} %get-tuple-element.52, f32[1536]{0:T(1024)} %get-tuple-element.53, f32[1536]{0:T(1024)} %get-tuple-element.6, f32[1536]{0:T(1024)} %get-tuple-element.7, f32[1536]{0:T(1024)} %get-tuple-element.8, ...), kind=kLoop, calls=%fused_computation.17 | loop fusion | flops 19660800 | bytes 39622656 | tf_op jit(solution)/shard_map/convert_element_type | solution.py:129
  (18 shorter events, 0.1 us)
Async XLA Ops:
  7.2 77.1 %all-gather.8.cloned.1.call-start = ((), (), s32[]{:S(2)}) async-start(), calls=%async_computation.6 | async-start | bytes 1253376 | tf_op jit(solution)/shard_map/all_gather | solution.py:79
  7.9 244.6 %all-gather.6.cloned.1.call-start = ((), (), s32[]{:S(2)}) async-start(), calls=%async_computation.5 | async-start | bytes 6684672 | tf_op jit(solution)/shard_map/all_gather | solution.py:83
  17.0 235.5 %copy-start.5 = (f32[384]{0:T(512)S(1)}, f32[384]{0:T(512)}, u32[]{:S(2)}) copy-start(f32[384]{0:T(512)} %param.14) | copy-start | bytes 4612
  17.0 271.1 %all-to-all-start = ((bf16[16,128,1536]{2,1,0:T(8,128)(2,1)}), bf16[16,128,1536]{2,1,0:T(8,128)(2,1)}, u32[]{:S(2)}, u32[]{:S(2)}) async-start(bf16[16,128,1536]{2,1,0:T(8,128)(2,1)} %stack.2), calls=%async_computation | async-start | bytes 12582912 | tf_op jit(solution)/shard_map/all_to_all | solution.py:85
  28.6 259.5 %all-gather.4.cloned.1.call-start = ((), (), s32[]{:S(2)}) async-start(), calls=%async_computation.4 | async-start | bytes 1253376 | tf_op jit(solution)/shard_map/all_gather | solution.py:80
  29.3 381.5 %reduce-scatter.4.cloned.1.call-start = ((), (), s32[]{:S(2)}) async-start(), calls=%async_computation.7 | async-start | bytes 6684672 | tf_op jit(solution)/shard_map/reduce_scatter | solution.py:106
  288.1 8.4 %copy-start.4 = (bf16[1536,384]{1,0:T(8,128)(2,1)S(1)}, bf16[1536,384]{1,0:T(8,128)(2,1)}, u32[]{:S(2)}) copy-start(bf16[1536,384]{1,0:T(8,128)(2,1)} %all-gather.8.cloned.1.call-done) | copy-start | bytes 3538948
  301.9 177.3 %reduce-scatter.6.cloned.1.call-start = ((), (), s32[]{:S(2)}) async-start(), calls=%async_computation.8 | async-start | bytes 2506752 | tf_op jit(solution)/shard_map/reduce_scatter | solution.py:115
  309.9 8.8 %copy-start.2 = (f32[7,7,1536]{2,1,0:T(8,128)S(1)}, f32[7,7,1536]{2,1,0:T(8,128)}, u32[]{:S(2)}) copy-start(f32[7,7,1536]{2,1,0:T(8,128)} %param.17) | copy-start | bytes 903172
  309.9 100.9 %copy-start.3 = (f32[1536]{0:T(1024)S(1)}, f32[1536]{0:T(1024)}, u32[]{:S(2)}) copy-start(f32[1536]{0:T(1024)} %param.11) | copy-start | bytes 18436
  309.9 239.4 %reduce-scatter.8.cloned.1.call-start = ((), (), s32[]{:S(2)}) async-start(), calls=%async_computation.9 | async-start | bytes 2506752 | tf_op jit(solution)/shard_map/reduce_scatter | solution.py:116
  318.6 92.2 %copy-start = (bf16[8,16,1536]{2,1,0:T(8,128)(2,1)S(1)}, bf16[8,16,1536]{2,1,0:T(8,128)(2,1)}, u32[]{:S(2)}) copy-start(bf16[8,16,1536]{2,1,0:T(8,128)(2,1)} %param.9) | copy-start | bytes 1179652
  412.1 139.1 %copy-start.1 = (bf16[8,16,1536]{2,1,0:T(8,128)(2,1)S(1)}, bf16[8,16,1536]{2,1,0:T(8,128)(2,1)}, u32[]{:S(2)}) copy-start(bf16[8,16,1536]{2,1,0:T(8,128)(2,1)} %param.10) | copy-start | bytes 1179652
  413.5 67.3 %collective-permute-start = (bf16[3,16,1536]{2,1,0:T(8,128)(2,1)S(1)}, bf16[3,16,1536]{2,1,0:T(8,128)(2,1)S(1)}, u32[]{:S(2)}, u32[]{:S(2)}) collective-permute-start(bf16[3,16,1536]{2,1,0:T(8,128)(2,1)S(1)} %bitcast.30), channel_id=1, source_target_pairs={{0,16},{16,32},{32,48},{48,64},{64,80},{80,96},{96,112},{112,128},... | collective-permute-start | bytes 442376 | tf_op jit(solution)/shard_map/ppermute | solution.py:17
  414.8 66.0 %collective-permute-start.1 = (bf16[3,16,1536]{2,1,0:T(8,128)(2,1)S(1)}, bf16[3,16,1536]{2,1,0:T(8,128)(2,1)S(1)}, u32[]{:S(2)}, u32[]{:S(2)}) collective-permute-start(bf16[3,16,1536]{2,1,0:T(8,128)(2,1)S(1)} %bitcast.29), channel_id=1, source_target_pairs={{16,0},{32,16},{48,32},{64,48},{80,64},{96,80},{112,96},{128,112},... | collective-permute-start | bytes 442376 | tf_op jit(solution)/shard_map/ppermute | solution.py:20
  480.9 69.9 %collective-permute-start.2 = (bf16[14,3,1536]{2,1,0:T(4,128)(2,1)S(1)}, bf16[14,3,1536]{2,1,0:T(4,128)(2,1)S(1)}, u32[]{:S(2)}, u32[]{:S(2)}) collective-permute-start(bf16[14,3,1536]{2,1,0:T(4,128)(2,1)S(1)} %get-tuple-element.54), channel_id=1, source_target_pairs={{0,1},{1,2},{2,3},{3,4},{4,5},{5,6},{6,7},{7,8},{8,9},{9,10},{10,1... | collective-permute-start | bytes 387080 | tf_op jit(solution)/shard_map/ppermute | solution.py:17
  485.6 65.3 %collective-permute-start.3 = (bf16[14,3,1536]{2,1,0:T(4,128)(2,1)S(1)}, bf16[14,3,1536]{2,1,0:T(4,128)(2,1)S(1)}, u32[]{:S(2)}, u32[]{:S(2)}) collective-permute-start(bf16[14,3,1536]{2,1,0:T(4,128)(2,1)S(1)} %get-tuple-element.55), channel_id=1, source_target_pairs={{1,0},{2,1},{3,2},{4,3},{5,4},{6,5},{7,6},{8,7},{9,8},{10,9},{11,1... | collective-permute-start | bytes 387080 | tf_op jit(solution)/shard_map/ppermute | solution.py:20
Sparse Core Ops, SparseCore 0:
  9.8 74.3 all-gather.7
  87.3 165.1 all-gather.5
  254.3 33.7 all-gather.3
  302.0 108.7 reduce-scatter.3
  413.2 65.9 reduce-scatter.5
  481.6 67.6 reduce-scatter.7
